TPU v7x, 512 devices: a whole 4x8x8 slice. The times are simulated.
512 devices in a mesh: grp: 16 (over z, core), dom: 32 (over x, y).
Axes of the slice: x: 4, y: 8, z: 8, core: 2. Of those that a mesh axis runs over, the one named last changes fastest.
Arguments:
- leaf_load: bfloat16 [32, 16, 1024, 128], P('dom', 'grp'), may hold values from -6 to 6
- leaf_map: bfloat16 [32, 16, 1024, 1024], P('dom', 'grp'), may hold values from -0.1875 to 0.1875
- group_map: bfloat16 [32, 4096, 4096], P('dom', 'grp'), may hold values from -0.09375 to 0.09375
- node_index: int32 [32, 16, 1024], P('dom', 'grp'), may hold values from 0 to 4095, as said below
- west_coupling: float32 [32, 256, 256], P('dom'), may hold values from -1.5 to 1.5
- east_coupling: float32 [32, 256, 256], P('dom'), may hold values from -1.5 to 1.5
Outputs:
- leaf_solution: bfloat16 [32, 16, 1024, 128], P('dom', 'grp')
Inputs may be any that keep to these rules, and one draw needn't show every extreme that they name: `node_index`: each leaf's list names 1024 different interface nodes of its group.
All inputs are finite; a program needn't handle non-finite values.
Results may differ from a plain program's by a relative error of at most 0.015.
Values may be sent and summed in bfloat16 or wider, within the bound.
No kernel may reach another device: no remote copies, remote signals or barrier semaphores. Data moves between devices by JAX's collectives and lax.ppermute only.
A program may use at most 128 MiB of HBM per device.

v0:
```python
import jax
import jax.numpy as jnp
from jax import lax
from jax.sharding import PartitionSpec as P


def carried_in(part, axis, combine, identity, reverse):
    count = lax.axis_size(axis)
    place = lax.axis_index(axis)
    ahead = count - 1 - place if reverse else place
    gathered = jax.tree.map(lambda a: lax.all_gather(a, axis), part)
    state = jax.tree.map(lambda a, e: jnp.zeros_like(a) + jnp.asarray(e, a.dtype), part, identity)

    def one(turn, state):
        source = count - 1 - turn if reverse else turn
        return combine(
            state, jax.tree.map(lambda a: lax.dynamic_index_in_dim(a, source, 0, False), gathered)
        )

    return lax.fori_loop(0, ahead, one, state)


def compose(earlier, follower):
    early_map, early_value = earlier
    late_map, late_value = follower
    joined_map = jnp.dot(
        late_map, early_map, precision=lax.Precision.HIGHEST, preferred_element_type=jnp.float32
    )
    joined_value = (
        jnp.dot(
            late_map,
            early_value,
            precision=lax.Precision.HIGHEST,
            preferred_element_type=jnp.float32,
        )
        + late_value
    )
    return (joined_map, joined_value)


def on_device(leaf_load, leaf_map, group_map, node_index, west_coupling, east_coupling):
    exact_mode = lax.Precision.HIGHEST
    columns = leaf_load.shape[3]
    interface = group_map.shape[2]
    face_nodes = west_coupling.shape[1]
    stride = interface // face_nodes
    local_map = leaf_map[0, 0]
    local_load = leaf_load[0, 0]
    local_index = node_index[0, 0]
    contrib = jnp.dot(local_map, local_load, preferred_element_type=jnp.float32).astype(
        jnp.bfloat16
    )
    scattered = (
        jnp.zeros((interface, columns), jnp.float32)
        .at[local_index]
        .add(contrib.astype(jnp.float32))
    )
    summed_loads = lax.psum(scattered.astype(jnp.bfloat16), "grp")
    rows_map = group_map[0]
    row_count = rows_map.shape[0]
    blocks = row_count // stride
    initial_rows = jnp.dot(rows_map, summed_loads, preferred_element_type=jnp.float32)
    block_view = rows_map.reshape(blocks, stride, face_nodes, stride)
    column_view = rows_map.reshape(row_count, face_nodes, stride)
    west_columns = column_view[:, :, 0].astype(jnp.float32)
    east_columns = column_view[:, :, 1].astype(jnp.float32)
    east_west = block_view[:, 1, :, 0].astype(jnp.float32)
    west_east = block_view[:, 0, :, 1].astype(jnp.float32)
    identity_map = jnp.eye(face_nodes, dtype=jnp.float32)
    zero_values = jnp.zeros((face_nodes, columns), jnp.float32)
    forward_maps = jnp.dot(east_west, west_coupling[0], precision=exact_mode)
    east_values = initial_rows.reshape(blocks, stride, columns)[:, 1]
    face_maps, face_values = (
        lax.all_gather(forward_maps, "grp", axis=0, tiled=True),
        lax.all_gather(east_values, "grp", axis=0, tiled=True),
    )
    _, incoming = carried_in(
        (face_maps, face_values), "dom", compose, (identity_map, zero_values), False
    )
    swept_rows = initial_rows + jnp.dot(
        west_columns,
        jnp.dot(west_coupling[0], incoming, precision=exact_mode),
        precision=exact_mode,
    )
    backward_maps = jnp.dot(west_east, east_coupling[0], precision=exact_mode)
    west_values = swept_rows.reshape(blocks, stride, columns)[:, 0]
    back_maps, back_values = (
        lax.all_gather(backward_maps, "grp", axis=0, tiled=True),
        lax.all_gather(west_values, "grp", axis=0, tiled=True),
    )
    _, outgoing = carried_in(
        (back_maps, back_values), "dom", compose, (identity_map, zero_values), True
    )
    final_rows = swept_rows + jnp.dot(
        east_columns,
        jnp.dot(east_coupling[0], outgoing, precision=exact_mode),
        precision=exact_mode,
    )
    gathered = lax.all_gather(final_rows.astype(jnp.bfloat16), "grp", axis=0, tiled=True)
    picked = gathered[local_index]
    result = lax.dot_general(
        local_map, picked, (((0,), (0,)), ((), ())), preferred_element_type=jnp.float32
    )
    result = result + local_load.astype(jnp.float32)
    return result.astype(jnp.bfloat16)[None, None]


def solution(mesh):
    return jax.shard_map(
        on_device,
        mesh=mesh,
        in_specs=(
            P("dom", "grp", None, None),
            P("dom", "grp", None, None),
            P("dom", "grp", None),
            P("dom", "grp", None),
            P("dom", None, None),
            P("dom", None, None),
        ),
        out_specs=P("dom", "grp", None, None),
        check_vma=False,
    )
```

profile of v0, /device:TPU:1, one launch (start us, length us, event | category | flops | bytes accessed | tf_op | source)
XLA Modules:
  0.0 639.1 jit_solution(5721224680582235260)
XLA Ops:
  6.5 0.8 compare_select_fusion
  7.4 0.8 copy-done
  8.1 1.6 fusion.21
  9.8 7.4 %scatter_custom_fusion = f32[4096,128]{1,0:T(8,128)} fusion(s32[1024]{0:T(1024)S(1)} %bitcast.114, f32[1024,128]{1,0:T(8,128)S(1)} %fusion.21, f32[]{:T(128)} %constant.56.clone.1), kind=kCustom, calls=%fused_computation.30 | custom fusion | flops 131072 | bytes 2097156 | tf_op jit(solution)/shard_map/scatter-add | solution.py:56
  17.2 2.7 convert_element_type.25
  20.0 123.9 %all-reduce.2.cloned.1.call-done = bf16[4096,128]{1,0:T(8,128)(2,1)} async-done(((bf16[4096,128]{1,0:T(8,128)(2,1)}), bf16[4096,128]{1,0:T(8,128)(2,1)}) %all-reduce.2.cloned.1.call-update) | async-done | bytes 1048592 | tf_op jit(solution)/shard_map/psum | solution.py:58
  143.9 2.7 fusion.30
  146.8 16.8 %all-gather.1 = f32[256,1,128]{2,1,0:T(1,128)} all-gather(f32[16,1,128]{2,1,0:T(1,128)S(1)} %slice.27), channel_id=3, replica_groups=mesh['grp'=16,'dom'=32] {'grp'}, dimensions={0}, use_global_device_ids=true | all-gather | bytes 139264 | tf_op jit(solution)/shard_map/all_gather | solution.py:75
  163.6 16.8 %reshape_squeeze.6 = bf16[16,16,256,16]{3,2,1,0:T(8,128)(2,1)} reshape(bf16[1,256,4096]{2,1,0:T(8,128)(2,1)} %param.12) | data formatting | bytes 4194304 | tf_op jit(solution)/shard_map/reshape;squeeze | solution.py:63
  180.4 2.6 slice_reduce_fusion
  183.0 0.2 fusion.45
  183.2 18.9 %all_gather.39 = f32[256,256]{1,0:T(8,128)} all-gather(f32[16,256]{1,0:T(8,128)S(1)} %fusion.45), channel_id=1, replica_groups=mesh['grp'=16,'dom'=32] {'grp'}, dimensions={0}, use_global_device_ids=true | all-gather | bytes 278528 | tf_op jit(solution)/shard_map/all_gather | solution.py:74
  202.2 0.2 fusion.41
  202.4 16.7 %all_gather.45 = f32[256,256]{1,0:T(8,128)} all-gather(f32[16,256]{1,0:T(8,128)S(1)} %fusion.41), channel_id=1, replica_groups=mesh['grp'=16,'dom'=32] {'grp'}, dimensions={0}, use_global_device_ids=true | all-gather | bytes 278528 | tf_op jit(solution)/shard_map/all_gather | solution.py:88
  219.2 4.1 copy.22
  223.3 2.0 fusion.49
  225.5 21.1 %all-gather.16.cloned.1.call-done = f32[8192,1,128]{2,1,0:T(1,128)} async-done(((f32[256,1,128]{2,1,0:T(1,128)}), f32[8192,1,128]{2,1,0:T(1,128)}) %all-gather.16.cloned.1.call-update) | async-done | bytes 4194320 | tf_op jit(solution)/shard_map/all_gather | solution.py:11
  246.6 106.2 %all-gather.14.cloned.1.call-done = f32[8192,256]{1,0:T(8,128)} async-done(((f32[256,256]{1,0:T(8,128)}), f32[8192,256]{1,0:T(8,128)}) %all-gather.14.cloned.1.call-update) | async-done | bytes 8388624 | tf_op jit(solution)/shard_map/all_gather | solution.py:11
  352.8 0.4 fusion.43
  353.2 0.3 fusion.33
  353.6 21.1 %all-gather.4 = f32[256,1,128]{2,1,0:T(1,128)} all-gather(f32[16,1,128]{2,1,0:T(1,128)S(1)} %slice.30), channel_id=6, replica_groups=mesh['grp'=16,'dom'=32] {'grp'}, dimensions={0}, use_global_device_ids=true | all-gather | bytes 139264 | tf_op jit(solution)/shard_map/all_gather | solution.py:89
  374.7 0.1 copy.25
  374.9 81.4 %all-gather.18.cloned.1.call-done = f32[8192,256]{1,0:T(8,128)} async-done(((f32[256,256]{1,0:T(8,128)}), f32[8192,256]{1,0:T(8,128)}) %all-gather.18.cloned.1.call-update) | async-done | bytes 8388624 | tf_op jit(solution)/shard_map/all_gather | solution.py:11
  456.3 84.8 %all-gather.20.cloned.1.call-done = f32[8192,1,128]{2,1,0:T(1,128)} async-done(((f32[256,1,128]{2,1,0:T(1,128)}), f32[8192,1,128]{2,1,0:T(1,128)}) %all-gather.20.cloned.1.call-update) | async-done | bytes 4194320 | tf_op jit(solution)/shard_map/all_gather | solution.py:11
  541.1 43.8 %while.27 = (s32[]{:T(128)}, f32[256,128]{1,0:T(8,128)S(1)}, s32[]{:T(128)}, f32[32,256,256]{2,1,0:T(8,128)}, f32[32,256,128]{2,1,0:T(8,128)}, /*index=5*/s32[]{:T(128)}, s32[]{:T(128)}, s32[]{:T(128)}, s32[]{:T(128)}) while((s32[]{:T(128)}, f32[256,128]{1,0:T(8,128)S(1)}, s32[]{:T(128)}, f32[32,256,256]{2,1,0:T(8,128)}, ...), condition=%wide.region_5.6_spmd, body=%wide.region_4.5_spmd.sunk | while | flops 100696072 | bytes 918675 | solution.py:20
  541.1 1.4 convolution_add_fusion.5
  542.6 1.4 convolution_add_fusion.5
  544.0 1.4 convolution_add_fusion.5
  545.4 1.4 convolution_add_fusion.5
  546.8 1.4 convolution_add_fusion.5
  548.2 1.4 convolution_add_fusion.5
  549.6 1.4 convolution_add_fusion.5
  551.1 1.4 convolution_add_fusion.5
  552.5 1.4 convolution_add_fusion.5
  553.9 1.4 convolution_add_fusion.5
  555.3 1.4 convolution_add_fusion.5
  556.7 1.4 convolution_add_fusion.5
  558.1 1.4 convolution_add_fusion.5
  559.5 1.4 convolution_add_fusion.5
  560.9 1.4 convolution_add_fusion.5
  562.3 1.4 convolution_add_fusion.5
  563.8 1.4 convolution_add_fusion.5
  565.2 1.4 convolution_add_fusion.5
  566.6 1.4 convolution_add_fusion.5
  568.0 1.4 convolution_add_fusion.5
  569.4 1.4 convolution_add_fusion.5
  570.8 1.4 convolution_add_fusion.5
  572.2 1.4 convolution_add_fusion.5
  573.6 1.4 convolution_add_fusion.5
  575.1 1.4 convolution_add_fusion.5
  576.5 1.4 convolution_add_fusion.5
  577.9 1.4 convolution_add_fusion.5
  579.3 1.4 convolution_add_fusion.5
  580.7 1.4 convolution_add_fusion.5
  582.1 1.4 convolution_add_fusion.5
  583.5 1.4 convolution_add_fusion.5
  584.9 0.4 fusion.39
  585.3 0.9 fusion.35
  586.3 0.9 copy.20
  587.1 38.1 %all-gather.12.cloned.1.call-done = bf16[4096,128]{0,1:T(8,128)(2,1)} async-done(((bf16[256,128]{0,1:T(8,128)(2,1)}), bf16[4096,128]{0,1:T(8,128)(2,1)}) %all-gather.12.cloned.1.call-update) | async-done | bytes 1048592 | tf_op jit(solution)/shard_map/all_gather | solution.py:99
  625.2 1.6 copy.26
  626.8 3.2 gather_fusion
  630.0 1.4 fusion.27
  631.5 0.8 copy.27
  (59 shorter events, 1.0 us)
Async XLA Ops:
  6.5 1.6 copy-start
  6.5 137.4 %all-reduce.2.cloned.1.call-start = ((), (), s32[]{:S(2)}) async-start(), calls=%async_computation | async-start | bytes 2097152 | tf_op jit(solution)/shard_map/psum | solution.py:58
  19.9 226.7 %all-gather.16.cloned.1.call-start = ((), (), s32[]{:S(2)}) async-start(), calls=%async_computation.3 | async-start | bytes 4325376 | tf_op jit(solution)/shard_map/all_gather | solution.py:11
  163.5 189.2 %all-gather.14.cloned.1.call-start = ((), (), s32[]{:S(2)}) async-start(), calls=%async_computation.2 | async-start | bytes 8650752 | tf_op jit(solution)/shard_map/all_gather | solution.py:11
  180.4 2.6 copy-start.1
  180.4 21.8 %copy-start.2 = (f32[1,256,256]{2,1,0:T(8,128)S(1)}, f32[1,256,256]{2,1,0:T(8,128)}, u32[]{:S(2)}) copy-start(f32[1,256,256]{2,1,0:T(8,128)} %param.15) | copy-start | bytes 786436
  202.1 254.1 %all-gather.18.cloned.1.call-start = ((), (), s32[]{:S(2)}) async-start(), calls=%async_computation.4 | async-start | bytes 8650752 | tf_op jit(solution)/shard_map/all_gather | solution.py:11
  219.1 321.9 %all-gather.20.cloned.1.call-start = ((), (), s32[]{:S(2)}) async-start(), calls=%async_computation.5 | async-start | bytes 4325376 | tf_op jit(solution)/shard_map/all_gather | solution.py:11
  374.7 250.5 %all-gather.12.cloned.1.call-start = ((), (), s32[]{:S(2)}) async-start(), calls=%async_computation.1 | async-start | bytes 1114112 | tf_op jit(solution)/shard_map/all_gather | solution.py:99
  541.1 45.2 %copy-start.3 = (bf16[1,1,1024,128]{3,2,1,0:T(8,128)(2,1)S(1)}, bf16[1,1,1024,128]{3,2,1,0:T(8,128)(2,1)}, u32[]{:S(2)}) copy-start(bf16[1,1,1024,128]{3,2,1,0:T(8,128)(2,1)} %param.10) | copy-start | bytes 786436
Sparse Core Ops, SparseCore 0:
  20.0 123.8 all-reduce.1
  163.7 82.8 all-gather.15
  249.8 102.9 all-gather.13
  355.8 100.4 all-gather.17
  459.3 81.7 all-gather.19
  586.4 38.7 all-gather.11
where the time goes:
time: 641 us; the launch traced here: 639 us
  waiting for transfers between devices  456 us (71%)
  blocking collectives  73.4 us (11%)
  matrix products  50.6 us (8%)
  local copies, waits for them, and re-layouts  33.6 us (5%)
  between operations  13.6 us (2%)
  other arithmetic  10.9 us (2%)
    all_gather x4, waiting for transfers between devices, carried_in(): gathered = jax.tree.map(lambda a: lax.all_gather(a, axis), part)  293 us
    psum x1, waiting for transfers between devices, on_device(): summed_loads = lax.psum(scattered.astype(jnp.bfloat16), 'grp')  124 us
    dot_general x31, matrix products, compose(): jnp.dot(late_map, early_value, precision=lax.Precision.HIGHEST, preferred...  42.3 us
    all_gather x1, waiting for transfers between devices, on_device(): lax.all_gather(final_rows.astype(jnp.bfloat16), 'grp', axis=0, tiled=True)  38.1 us
    all_gather x1, blocking collectives, on_device(): lax.all_gather(west_values, 'grp', axis=0, tiled=True)  21.1 us
    all_gather x1, blocking collectives, on_device(): lax.all_gather(forward_maps, 'grp', axis=0, tiled=True)  18.9 us
    another operation x1, local copies, waits for them, and re-layouts, on_device(): block_view = rows_map.reshape(blocks, stride, face_nodes, stride)  16.8 us
    all_gather x1, blocking collectives, on_device(): lax.all_gather(east_values, 'grp', axis=0, tiled=True)  16.8 us
  transfers between devices with their start and end apart: 6, of which 6 were waited for; matrix products, arithmetic and copies ran while one was open for 4% of the time, Pallas kernels for 0%

commit v1 on v0

--- a/solution.py
+++ b/solution.py
@@ -55,7 +55,7 @@
         .at[local_index]
         .add(contrib.astype(jnp.float32))
     )
-    summed_loads = lax.psum(scattered.astype(jnp.bfloat16), "grp")
+    summed_loads = jnp.sum(lax.all_gather(scattered.astype(jnp.bfloat16), "grp"), axis=0)
     rows_map = group_map[0]
     row_count = rows_map.shape[0]
     blocks = row_count // stride

time: 641 us -> 604 us (0.942)
  waiting for transfers between devices: 456 us -> 397 us
  blocking collectives: 73.4 us -> 86.5 us
  other arithmetic: 10.9 us -> 19.9 us
    psum x1 -> x0, waiting for transfers between devices: 124 us -> none  [on_device(): summed_loads = lax.psum(scattered.astype(jnp.bfloat16), 'grp')]
    all_gather x0 -> x1, waiting for transfers between devices: none -> 58 us  [on_device(): lax.all_gather(scattered.astype(jnp.bfloat16), 'grp')]
    all_gather x1, blocking collectives: 18.9 us -> 28.5 us  [on_device(): lax.all_gather(forward_maps, 'grp', axis=0, tiled=True)]
    reduce_sum x0 -> x1, other arithmetic: none -> 8.87 us  [on_device(): jnp.sum(lax.all_gather(scattered.astype(jnp.bfloat16), 'grp'), axis=0)]
    all_gather x4, waiting for transfers between devices: 293 us -> 301 us  [carried_in(): gathered = jax.tree.map(lambda a: lax.all_gather(a, axis), part)]
  transfers between devices with their start and end apart: 6 -> 6, of which waited for: 6 -> 6; matrix products, arithmetic and copies ran while one was open for 4% -> 7% of each run, Pallas kernels for 0% -> 0%
where the time goes in v1:
time: 604 us; the launch traced here: 603 us
  waiting for transfers between devices  397 us (66%)
  blocking collectives  86.5 us (14%)
  matrix products  51.2 us (8%)
  local copies, waits for them, and re-layouts  33.5 us (6%)
  other arithmetic  19.9 us (3%)
  between operations  13.7 us (2%)
    all_gather x4, waiting for transfers between devices, carried_in(): gathered = jax.tree.map(lambda a: lax.all_gather(a, axis), part)  301 us
    all_gather x1, waiting for transfers between devices, on_device(): lax.all_gather(scattered.astype(jnp.bfloat16), 'grp')  58 us
    dot_general x31, matrix products, compose(): jnp.dot(late_map, early_value, precision=lax.Precision.HIGHEST, preferred...  42.4 us
    all_gather x1, waiting for transfers between devices, on_device(): lax.all_gather(final_rows.astype(jnp.bfloat16), 'grp', axis=0, tiled=True)  38.1 us
    all_gather x1, blocking collectives, on_device(): lax.all_gather(forward_maps, 'grp', axis=0, tiled=True)  28.5 us
    all_gather x1, blocking collectives, on_device(): lax.all_gather(west_values, 'grp', axis=0, tiled=True)  23.8 us
    all_gather x1, blocking collectives, on_device(): lax.all_gather(east_values, 'grp', axis=0, tiled=True)  17.2 us
    all_gather x1, blocking collectives, on_device(): lax.all_gather(backward_maps, 'grp', axis=0, tiled=True)  17 us
  transfers between devices with their start and end apart: 6, of which 6 were waited for; matrix products, arithmetic and copies ran while one was open for 7% of the time, Pallas kernels for 0%

profile of v1, /device:TPU:1, one launch (start us, length us, event | category | flops | bytes accessed | tf_op | source)
XLA Modules:
  0.0 603.0 jit_solution(3223060665985337164)
XLA Ops:
  6.5 0.8 compare_select_fusion
  7.4 0.8 copy-done
  8.1 1.6 fusion.21
  9.8 7.4 %scatter_custom_fusion = f32[4096,128]{1,0:T(8,128)} fusion(s32[1024]{0:T(1024)S(1)} %bitcast.116, f32[1024,128]{1,0:T(8,128)S(1)} %fusion.21, f32[]{:T(128)} %constant.58.clone.1), kind=kCustom, calls=%fused_computation.30 | custom fusion | flops 131072 | bytes 2097156 | tf_op jit(solution)/shard_map/scatter-add | solution.py:56
  17.2 2.7 convert_element_type.27
  20.0 16.8 %reshape_squeeze.6 = bf16[16,16,256,16]{3,2,1,0:T(8,128)(2,1)} reshape(bf16[1,256,4096]{2,1,0:T(8,128)(2,1)} %param.12) | data formatting | bytes 4194304 | tf_op jit(solution)/shard_map/reshape;squeeze | solution.py:63
  36.8 2.6 slice_reduce_fusion
  39.4 0.2 fusion.45
  39.6 28.5 %all_gather.47 = f32[256,256]{1,0:T(8,128)} all-gather(f32[16,256]{1,0:T(8,128)S(1)} %fusion.45), channel_id=1, replica_groups=mesh['grp'=16,'dom'=32] {'grp'}, dimensions={0}, use_global_device_ids=true | all-gather | bytes 278528 | tf_op jit(solution)/shard_map/all_gather | solution.py:74
  68.1 58.0 %all-gather.16.cloned.1.call-done = bf16[65536,128]{1,0:T(8,128)(2,1)} async-done(((bf16[4096,128]{1,0:T(8,128)(2,1)}), bf16[65536,128]{1,0:T(8,128)(2,1)}) %all-gather.16.cloned.1.call-update) | async-done | bytes 16777232 | tf_op jit(solution)/shard_map/all_gather | solution.py:58
  126.2 8.9 %reduce_sum.12 = bf16[4096,128]{1,0:T(8,128)(2,1)S(1)} reduce(bf16[16,4096,128]{2,1,0:T(8,128)(2,1)} %bitcast.108, bf16[]{:T(256)} %constant.61.clone.1), dimensions={0}, to_apply=%region_1.0 | reduce | flops 7864320 | bytes 17825794 | tf_op jit(solution)/shard_map/reduce_sum | solution.py:58
  135.1 2.4 fusion.30
  137.6 17.2 %all-gather.2 = f32[256,1,128]{2,1,0:T(1,128)} all-gather(f32[16,1,128]{2,1,0:T(1,128)S(1)} %slice.27), channel_id=4, replica_groups=mesh['grp'=16,'dom'=32] {'grp'}, dimensions={0}, use_global_device_ids=true | all-gather | bytes 139264 | tf_op jit(solution)/shard_map/all_gather | solution.py:75
  154.9 1.2 fusion.41
  156.1 17.0 %all_gather.53 = f32[256,256]{1,0:T(8,128)} all-gather(f32[16,256]{1,0:T(8,128)S(1)} %fusion.41), channel_id=1, replica_groups=mesh['grp'=16,'dom'=32] {'grp'}, dimensions={0}, use_global_device_ids=true | all-gather | bytes 278528 | tf_op jit(solution)/shard_map/all_gather | solution.py:88
  173.1 4.1 copy.30
  177.2 2.0 fusion.49
  179.3 49.8 %all-gather.18.cloned.1.call-done = f32[8192,256]{1,0:T(8,128)} async-done(((f32[256,256]{1,0:T(8,128)}), f32[8192,256]{1,0:T(8,128)}) %all-gather.18.cloned.1.call-update) | async-done | bytes 8388624 | tf_op jit(solution)/shard_map/all_gather | solution.py:11
  229.1 84.9 %all-gather.20.cloned.1.call-done = f32[8192,1,128]{2,1,0:T(1,128)} async-done(((f32[256,1,128]{2,1,0:T(1,128)}), f32[8192,1,128]{2,1,0:T(1,128)}) %all-gather.20.cloned.1.call-update) | async-done | bytes 4194320 | tf_op jit(solution)/shard_map/all_gather | solution.py:11
  314.1 0.4 fusion.43
  314.5 0.3 fusion.33
  314.9 23.8 %all-gather.5 = f32[256,1,128]{2,1,0:T(1,128)} all-gather(f32[16,1,128]{2,1,0:T(1,128)S(1)} %slice.30), channel_id=7, replica_groups=mesh['grp'=16,'dom'=32] {'grp'}, dimensions={0}, use_global_device_ids=true | all-gather | bytes 139264 | tf_op jit(solution)/shard_map/all_gather | solution.py:89
  338.9 81.1 %all-gather.22.cloned.1.call-done = f32[8192,256]{1,0:T(8,128)} async-done(((f32[256,256]{1,0:T(8,128)}), f32[8192,256]{1,0:T(8,128)}) %all-gather.22.cloned.1.call-update) | async-done | bytes 8388624 | tf_op jit(solution)/shard_map/all_gather | solution.py:11
  420.0 84.8 %all-gather.24.cloned.1.call-done = f32[8192,1,128]{2,1,0:T(1,128)} async-done(((f32[256,1,128]{2,1,0:T(1,128)}), f32[8192,1,128]{2,1,0:T(1,128)}) %all-gather.24.cloned.1.call-update) | async-done | bytes 4194320 | tf_op jit(solution)/shard_map/all_gather | solution.py:11
  504.9 43.8 %while.27 = (s32[]{:T(128)}, f32[256,128]{1,0:T(8,128)S(1)}, s32[]{:T(128)}, f32[32,256,256]{2,1,0:T(8,128)}, f32[32,256,128]{2,1,0:T(8,128)}, /*index=5*/s32[]{:T(128)}, s32[]{:T(128)}, s32[]{:T(128)}, s32[]{:T(128)}) while((s32[]{:T(128)}, f32[256,128]{1,0:T(8,128)S(1)}, s32[]{:T(128)}, f32[32,256,256]{2,1,0:T(8,128)}, ...), condition=%wide.region_5.6_spmd, body=%wide.region_4.5_spmd.sunk | while | flops 100696072 | bytes 918675 | solution.py:20
  504.9 1.4 convolution_add_fusion.5
  506.4 1.4 convolution_add_fusion.5
  507.8 1.4 convolution_add_fusion.5
  509.2 1.4 convolution_add_fusion.5
  510.6 1.4 convolution_add_fusion.5
  512.0 1.4 convolution_add_fusion.5
  513.4 1.4 convolution_add_fusion.5
  514.8 1.4 convolution_add_fusion.5
  516.3 1.4 convolution_add_fusion.5
  517.7 1.4 convolution_add_fusion.5
  519.1 1.4 convolution_add_fusion.5
  520.5 1.4 convolution_add_fusion.5
  521.9 1.4 convolution_add_fusion.5
  523.3 1.4 convolution_add_fusion.5
  524.7 1.4 convolution_add_fusion.5
  526.1 1.4 convolution_add_fusion.5
  527.6 1.4 convolution_add_fusion.5
  529.0 1.4 convolution_add_fusion.5
  530.4 1.4 convolution_add_fusion.5
  531.8 1.4 convolution_add_fusion.5
  533.2 1.4 convolution_add_fusion.5
  534.6 1.4 convolution_add_fusion.5
  536.0 1.4 convolution_add_fusion.5
  537.4 1.4 convolution_add_fusion.5
  538.9 1.4 convolution_add_fusion.5
  540.3 1.4 convolution_add_fusion.5
  541.7 1.4 convolution_add_fusion.5
  543.1 1.4 convolution_add_fusion.5
  544.5 1.4 convolution_add_fusion.5
  545.9 1.4 convolution_add_fusion.5
  547.3 1.4 convolution_add_fusion.5
  548.7 0.4 fusion.39
  549.1 0.9 fusion.35
  550.1 0.9 copy.28
  550.9 38.1 %all-gather.14.cloned.1.call-done = bf16[4096,128]{0,1:T(8,128)(2,1)} async-done(((bf16[256,128]{0,1:T(8,128)(2,1)}), bf16[4096,128]{0,1:T(8,128)(2,1)}) %all-gather.14.cloned.1.call-update) | async-done | bytes 1048592 | tf_op jit(solution)/shard_map/all_gather | solution.py:99
  589.0 1.6 copy.34
  590.6 3.2 gather_fusion
  593.8 1.4 fusion.27
  595.3 0.8 copy.35
  (60 shorter events, 1.2 us)
Async XLA Ops:
  6.5 1.6 copy-start
  6.5 119.6 %all-gather.16.cloned.1.call-start = ((), (), s32[]{:S(2)}) async-start(), calls=%async_computation.1 | async-start | bytes 17825792 | tf_op jit(solution)/shard_map/all_gather | solution.py:58
  20.0 209.1 %all-gather.18.cloned.1.call-start = ((), (), s32[]{:S(2)}) async-start(), calls=%async_computation.2 | async-start | bytes 8650752 | tf_op jit(solution)/shard_map/all_gather | solution.py:11
  36.8 2.6 copy-start.1
  68.1 245.9 %all-gather.20.cloned.1.call-start = ((), (), s32[]{:S(2)}) async-start(), calls=%async_computation.3 | async-start | bytes 4325376 | tf_op jit(solution)/shard_map/all_gather | solution.py:11
  154.9 265.2 %all-gather.22.cloned.1.call-start = ((), (), s32[]{:S(2)}) async-start(), calls=%async_computation.4 | async-start | bytes 8650752 | tf_op jit(solution)/shard_map/all_gather | solution.py:11
  173.1 331.8 %all-gather.24.cloned.1.call-start = ((), (), s32[]{:S(2)}) async-start(), calls=%async_computation.5 | async-start | bytes 4325376 | tf_op jit(solution)/shard_map/all_gather | solution.py:11
  338.7 250.3 %all-gather.14.cloned.1.call-start = ((), (), s32[]{:S(2)}) async-start(), calls=%async_computation | async-start | bytes 1114112 | tf_op jit(solution)/shard_map/all_gather | solution.py:99
  504.8 43.9 %copy-start.2 = (f32[1,256,256]{2,1,0:T(8,128)S(1)}, f32[1,256,256]{2,1,0:T(8,128)}, u32[]{:S(2)}) copy-start(f32[1,256,256]{2,1,0:T(8,128)} %param.15) | copy-start | bytes 786436
  504.8 45.2 %copy-start.3 = (bf16[1,1,1024,128]{3,2,1,0:T(8,128)(2,1)S(1)}, bf16[1,1,1024,128]{3,2,1,0:T(8,128)(2,1)}, u32[]{:S(2)}) copy-start(bf16[1,1,1024,128]{3,2,1,0:T(8,128)(2,1)} %param.10) | copy-start | bytes 786436
Sparse Core Ops, SparseCore 0:
  20.1 106.0 all-gather.15
  129.4 99.6 all-gather.17
  232.3 81.7 all-gather.19
  317.1 102.9 all-gather.21
  423.1 81.7 all-gather.23
  550.2 38.7 all-gather.13
